TPU v7x, 32 devices: a whole 2x2x4 slice. The times are simulated.
32 devices in a mesh: grp: 2 (over y), occ: 4 (over z), aux: 2 (over x), vir: 2 (over core).
Axes of the slice: x: 2, y: 2, z: 4, core: 2. Of those that a mesh axis runs over, the one named last changes fastest.
Arguments:
- integrals: bfloat16 [4, 1024, 8, 1280], P('occ', 'aux', 'grp', 'vir'), parts along dimension 2, may hold values from -0.59765625 to 0.59765625
- occ_energy: float32 [8], P('grp'), parts along dimension 0, may hold values from -1.5 to -0.3
- vir_energy: float32 [2560], P('grp'), parts along dimension 0, may hold values from 0.2 to 3
- round_owner: int32 [4], P('grp'), parts along dimension 0, may hold values from 0 to 3, as said below
Outputs:
- gamma_field: float32 [8, 1024, 4, 1280], P('grp', 'aux', 'occ', 'vir'), parts along dimension 0
There are 2 independent parts, one for each index of `grp`. A program takes and returns all parts, laid end to end along the dimension named above; each array names one. Nothing has to cross between parts.
Inputs may be any that keep to these rules, and one draw needn't show every extreme that they name: `round_owner`: the 2 owners are distinct.
All inputs are finite; a program needn't handle non-finite values.
Results may differ from a plain program's by a relative error of at most 0.0085.
Values may be sent and summed in bfloat16 or wider, within the bound.
No kernel may reach another device: no remote copies, remote signals or barrier semaphores. Data moves between devices by JAX's collectives and lax.ppermute only.
A program may use at most 64 MiB of HBM per device.

v0:
```python
import jax
import jax.numpy as jnp
from jax import lax
from jax.sharding import PartitionSpec as P

ROUNDS = 2


def from_root(value, axis, root):
    mine = lax.axis_index(axis) == root
    return lax.psum(jnp.where(mine, value, jnp.zeros_like(value)), axis)


def local(integrals, occ_energy, vir_energy, round_owner):
    regrouped = lax.all_to_all(integrals, "occ", split_axis=2, concat_axis=0, tiled=True)
    occ_width = regrouped.shape[2]
    vir_width = regrouped.shape[3]
    energy_i = lax.dynamic_slice_in_dim(occ_energy, lax.axis_index("occ") * occ_width, occ_width)
    energy_a = lax.dynamic_slice_in_dim(vir_energy, lax.axis_index("vir") * vir_width, vir_width)
    gamma_total = jnp.zeros(regrouped.shape, jnp.float32)
    for turn_index in range(ROUNDS):
        owner = round_owner[turn_index]
        owner_half = from_root(regrouped, "occ", owner)
        owner_whole = lax.all_gather(owner_half, "vir", axis=3, tiled=True)
        energy_j = lax.dynamic_slice_in_dim(occ_energy, owner * occ_width, occ_width)
        partial_value = jnp.einsum(
            "sria,srjb->ijab", regrouped, owner_whole, preferred_element_type=jnp.float32
        )
        base = energy_i[:, None, None] + energy_j[None, :, None] - energy_a[None, None, :]
        pair_block = lax.psum(partial_value.astype(jnp.bfloat16), "aux").astype(jnp.float32)
        amplitude = (pair_block / (base[..., None] - vir_energy)).astype(jnp.bfloat16)
        gamma_total = gamma_total + jnp.einsum(
            "ijab,srjb->sria", amplitude, owner_whole, preferred_element_type=jnp.float32
        )
    return gamma_total


def solution(mesh):
    placed = (P("occ", "aux", "grp", "vir"), P("grp"), P("grp"), P("grp"))
    return jax.shard_map(
        local, mesh=mesh, in_specs=placed, out_specs=P("grp", "aux", "occ", "vir"), check_vma=False
    )
```

profile of v0, /device:TPU:0, one launch (start us, length us, event | category | flops | bytes accessed | tf_op | source)
XLA Modules:
  0.0 432.3 jit_solution(8235440638298763735)
XLA Ops:
  6.5 3.6 copy.11
  10.1 0.0 copy-start.2
  10.1 6.4 %all-to-all-start = ((bf16[1,512,4,640]{3,1,0,2:T(8,128)(2,1)}), bf16[1,512,4,640]{3,1,0,2:T(8,128)(2,1)S(1)}, u32[]{:S(2)}, u32[]{:S(2)}) async-start(bf16[1,512,4,640]{3,1,0,2:T(8,128)(2,1)} %copy.11), calls=%async_computation | async-start | bytes 5242880 | tf_op jit(solution)/shard_map/all_to_all | solution.py:15
  16.5 0.0 all-reduce.5.cloned.1.call-start
  16.5 0.0 copy-done.2
  16.6 0.7 fusion.41
  18.5 57.4 %all-to-all-done = bf16[1,512,4,640]{3,1,0,2:T(8,128)(2,1)S(1)} async-done(((bf16[1,512,4,640]{3,1,0,2:T(8,128)(2,1)}), bf16[1,512,4,640]{3,1,0,2:T(8,128)(2,1)S(1)}, u32[]{:S(2)}, u32[]{:S(2)}) %all-to-all-start) | async-done | bytes 2621472 | tf_op jit(solution)/shard_map/all_to_all | solution.py:15
  76.0 2.8 fusion.28
  78.8 0.0 all-reduce.5.cloned.1.call-update
  78.8 0.0 all-gather.3.cloned.1.call-start
  78.8 188.5 %all-reduce.5.cloned.1.call-done = (bf16[4,512,1,640]{3,1,0,2:T(8,128)(2,1)}, bf16[4,512,1,640]{3,1,0,2:T(8,128)(2,1)}) async-done(((bf16[4,512,1,640]{3,1,0,2:T(8,128)(2,1)}, bf16[4,512,1,640]{3,1,0,2:T(8,128)(2,1)}), (bf16[4,512,1,640]{3,1,0,2:T(8,128)(2,1)}, bf16[4,512,1,640]{3,1,0,2:T(8,128)(2,1)})) %all-reduce.5.cloned.1.call-update) | async-done | bytes 5242896 | tf_op jit(solution)/shard_map/psum | solution.py:11
  267.3 0.0 all-gather.3.cloned.1.call-update
  267.4 0.0 all-gather.5.cloned.1.call-start
  267.4 0.7 all-gather.5.cloned.1.call-update
  268.1 0.0 all-reduce.7.cloned.1.call-start
  268.1 14.9 %all-gather.3.cloned.1.call-done = bf16[4,512,1,1280]{3,1,0,2:T(8,128)(2,1)} async-done(((bf16[4,512,1,640]{3,1,0,2:T(8,128)(2,1)}), bf16[4,512,1,1280]{3,1,0,2:T(8,128)(2,1)}) %all-gather.3.cloned.1.call-update) | async-done | bytes 5242896 | tf_op jit(solution)/shard_map/all_gather | solution.py:24
  283.0 8.0 %fusion.20 = bf16[1,1,640,1280]{2,3,0,1:T(8,128)(2,1)} fusion(bf16[4,512,1,1280]{3,1,0,2:T(8,128)(2,1)} %all-gather.3.cloned.1.call-done, bf16[1,512,4,640]{3,1,0,2:T(8,128)(2,1)S(1)} %all-to-all-done), kind=kOutput, calls=%fused_computation.15 | convolution fusion | flops 3356262400 | bytes 9502720 | tf_op jit(solution)/shard_map/sria,srjb->ijab/dot_general | solution.py:26
  291.0 9.9 %all-gather.5.cloned.1.call-done = bf16[4,512,1,1280]{3,1,0,2:T(8,128)(2,1)} async-done(((bf16[4,512,1,640]{3,1,0,2:T(8,128)(2,1)}), bf16[4,512,1,1280]{3,1,0,2:T(8,128)(2,1)}) %all-gather.5.cloned.1.call-update) | async-done | bytes 5242896 | tf_op jit(solution)/shard_map/all_gather | solution.py:24
  300.9 8.0 %fusion.23 = bf16[1,1,640,1280]{2,3,0,1:T(8,128)(2,1)} fusion(bf16[4,512,1,1280]{3,1,0,2:T(8,128)(2,1)} %all-gather.5.cloned.1.call-done, bf16[1,512,4,640]{3,1,0,2:T(8,128)(2,1)S(1)} %all-to-all-done), kind=kOutput, calls=%fused_computation.16 | convolution fusion | flops 3356262400 | bytes 9502720 | tf_op jit(solution)/shard_map/sria,srjb->ijab/dot_general | solution.py:26
  308.8 0.0 copy-start
  308.9 0.0 copy-start.1
  308.9 0.0 all-reduce.7.cloned.1.call-update
  312.8 0.0 copy-done
  312.9 0.7 fusion.40
  316.0 0.0 copy-done.1
  316.0 0.1 dynamic-slice_subtract_fusion.1
  316.1 82.9 %all-reduce.7.cloned.1.call-done = (bf16[1,1,640,1280]{2,3,0,1:T(8,128)(2,1)}, bf16[1,1,640,1280]{2,3,0,1:T(8,128)(2,1)}) async-done(((bf16[1,1,640,1280]{2,3,0,1:T(8,128)(2,1)}, bf16[1,1,640,1280]{2,3,0,1:T(8,128)(2,1)}), (bf16[1,1,640,1280]{2,3,0,1:T(8,128)(2,1)}, bf16[1,1,640,1280]{2,3,0,1:T(8,128)(2,1)})) %all-reduce.7.cloned.1.call-update) | async-done | bytes 3276816 | tf_op jit(solution)/shard_map/psum | solution.py:30
  399.0 0.0 copy-start.3
  399.0 7.2 %fusion = f32[4,512,640]{2,1,0:T(8,128)S(1)} fusion(bf16[4,512,1,1280]{3,1,0,2:T(8,128)(2,1)} %all-gather.5.cloned.1.call-done, bf16[1,1,640,1280]{2,3,0,1:T(8,128)(2,1)} %get-tuple-element.7, f32[640]{0:T(1024)S(1)} %get-tuple-element.12, f32[1280]{0:T(1024)S(1)} %copy-done.1), kind=kOutput, calls=%fused_computation | convolution fusion | flops 3358720000 | bytes 12131840 | tf_op jit(solution)/shard_map/ijab,srjb->sria/dot_general | solution.py:32
  406.2 0.0 copy-done.3
  406.2 9.3 %add_bitcast_fusion = f32[4,512,1,640]{3,1,0,2:T(8,128)} fusion(f32[4,512,640]{2,1,0:T(8,128)S(1)} %fusion, bf16[4,512,1,1280]{3,1,0,2:T(8,128)(2,1)} %all-gather.3.cloned.1.call-done, bf16[1,1,640,1280]{2,3,0,1:T(8,128)(2,1)S(1)} %copy-done.3, f32[1280]{0:T(1024)S(1)} %copy-done.1, f32[640]{0:T(1024)S(1)} %get-tuple-element.11), kind=kOutput, calls=%fused_computation.8 | convolution fusion | flops 3360030720 | bytes 17374720 | tf_op jit(solution)/shard_map/ijab,srjb->sria/dot_general | solution.py:32
  415.5 10.2 %copy.16 = f32[4,512,1,640]{3,2,1,0:T(1,128)} copy(f32[4,512,1,640]{3,1,0,2:T(8,128)} %add_bitcast_fusion) | data formatting | bytes 10485760 | tf_op jit(solution)/shard_map/add | solution.py:32
Async XLA Ops:
  10.1 6.5 %copy-start.2 = (s32[2]{0:T(128)S(1)}, s32[2]{0:T(128)}, u32[]{:S(2)}) copy-start(s32[2]{0:T(128)} %param.7) | copy-start | bytes 28
  10.1 65.9 %all-to-all-start = ((bf16[1,512,4,640]{3,1,0,2:T(8,128)(2,1)}), bf16[1,512,4,640]{3,1,0,2:T(8,128)(2,1)S(1)}, u32[]{:S(2)}, u32[]{:S(2)}) async-start(bf16[1,512,4,640]{3,1,0,2:T(8,128)(2,1)} %copy.11), calls=%async_computation | async-start | bytes 5242880 | tf_op jit(solution)/shard_map/all_to_all | solution.py:15
  16.5 250.8 %all-reduce.5.cloned.1.call-start = ((), (), s32[]{:S(2)}) async-start(), calls=%async_computation.3 | async-start | bytes 10485760 | tf_op jit(solution)/shard_map/psum | solution.py:11
  78.8 204.2 %all-gather.3.cloned.1.call-start = ((), (), s32[]{:S(2)}) async-start(), calls=%async_computation.1 | async-start | bytes 7864320 | tf_op jit(solution)/shard_map/all_gather | solution.py:24
  267.4 33.5 %all-gather.5.cloned.1.call-start = ((), (), s32[]{:S(2)}) async-start(), calls=%async_computation.2 | async-start | bytes 7864320 | tf_op jit(solution)/shard_map/all_gather | solution.py:24
  268.1 130.9 %all-reduce.7.cloned.1.call-start = ((), (), s32[]{:S(2)}) async-start(), calls=%async_computation.4 | async-start | bytes 6553600 | tf_op jit(solution)/shard_map/psum | solution.py:30
  308.8 4.0 copy-start
  308.9 7.1 %copy-start.1 = (f32[1280]{0:T(1024)S(1)}, f32[1280]{0:T(1024)}, u32[]{:S(2)}) copy-start(f32[1280]{0:T(1024)} %param.6) | copy-start | bytes 15364
  399.0 7.2 %copy-start.3 = (bf16[1,1,640,1280]{2,3,0,1:T(8,128)(2,1)S(1)}, bf16[1,1,640,1280]{2,3,0,1:T(8,128)(2,1)}, u32[]{:S(2)}) copy-start(bf16[1,1,640,1280]{2,3,0,1:T(8,128)(2,1)} %get-tuple-element.8) | copy-start | bytes 4915204
Sparse Core Ops, SparseCore 0:
  78.9 188.3 all-reduce.4
  268.9 14.0 all-gather.2
  284.6 16.2 all-gather.4
  309.0 89.9 all-reduce.6
where the time goes:
time: 433 us; the launch traced here: 432 us
  waiting for transfers between devices  354 us (82%)
  matrix products  32.4 us (7%)
  between operations  20.9 us (5%)
  local copies, waits for them, and re-layouts  15.1 us (3%)
  starting transfers between devices  6.57 us (2%)
    psum x1, waiting for transfers between devices, from_root(): return lax.psum(jnp.where(mine, value, jnp.zeros_like(value)), axis)  188 us
    psum x1, waiting for transfers between devices, local(): lax.psum(partial_value.astype(jnp.bfloat16), 'aux').astype(jnp.float32)  82.9 us
    all_to_all x1, waiting for transfers between devices, local(): lax.all_to_all(integrals, 'occ', split_axis=2, concat_axis=0, tiled=True)  57.4 us
    all_gather x2, waiting for transfers between devices, local(): owner_whole = lax.all_gather(owner_half, 'vir', axis=3, tiled=True)  24.8 us
    dot_general x2, matrix products, local(): jnp.einsum('ijab,srjb->sria', amplitude, owner_whole, preferred_element_t...  16.5 us
    dot_general x2, matrix products, local(): jnp.einsum('sria,srjb->ijab', regrouped, owner_whole, preferred_element_t...  15.9 us
    add x1, local copies, waits for them, and re-layouts, local(): gamma_total + jnp.einsum('ijab,srjb->sria', amplitude, owner_whole, prefe...  10.2 us
  transfers between devices with their start and end apart: 5, of which 5 were waited for; matrix products, arithmetic and copies ran while one was open for 2% of the time, Pallas kernels for 0%

commit v1 on v0

--- a/solution.py
+++ b/solution.py
@@ -27,7 +27,9 @@
             "sria,srjb->ijab", regrouped, owner_whole, preferred_element_type=jnp.float32
         )
         base = energy_i[:, None, None] + energy_j[None, :, None] - energy_a[None, None, :]
-        pair_block = lax.psum(partial_value.astype(jnp.bfloat16), "aux").astype(jnp.float32)
+        pair_block = jnp.sum(
+            lax.all_gather(partial_value.astype(jnp.bfloat16), "aux"), axis=0
+        ).astype(jnp.float32)
         amplitude = (pair_block / (base[..., None] - vir_energy)).astype(jnp.bfloat16)
         gamma_total = gamma_total + jnp.einsum(
             "ijab,srjb->sria", amplitude, owner_whole, preferred_element_type=jnp.float32

time: 433 us -> 438 us (1.012)
  waiting for transfers between devices: 354 us -> 340 us
  local copies, waits for them, and re-layouts: 15.1 us -> 26.9 us
  other arithmetic: 2.88 us -> 9.93 us
    psum x1 -> x0, waiting for transfers between devices: 82.9 us -> none  [local(): lax.psum(partial_value.astype(jnp.bfloat16), 'aux').astype(jnp.float32)]
    all_gather x0 -> x2, waiting for transfers between devices: none -> 72.3 us  [local(): lax.all_gather(partial_value.astype(jnp.bfloat16), 'aux')]
    convert_element_type x0 -> x2, local copies, waits for them, and re-layouts: none -> 7.43 us  [local(): partial_value.astype(jnp.bfloat16)]
    reduce_sum x0 -> x2, other arithmetic: none -> 7.04 us  [local(): jnp.sum(lax.all_gather(partial_value.astype(jnp.bfloat16), 'aux'), axis=0)]
    unnamed x9 -> x11, local copies, waits for them, and re-layouts: 3.57 us -> 7.98 us
  transfers between devices with their start and end apart: 5 -> 6, of which waited for: 5 -> 6; matrix products, arithmetic and copies ran while one was open for 2% -> 7% of each run, Pallas kernels for 0% -> 0%
where the time goes in v1:
time: 438 us; the launch traced here: 437 us
  waiting for transfers between devices  340 us (78%)
  matrix products  32.6 us (7%)
  local copies, waits for them, and re-layouts  26.9 us (6%)
  between operations  20.8 us (5%)
  other arithmetic  9.93 us (2%)
  starting transfers between devices  6.79 us (2%)
    psum x1, waiting for transfers between devices, from_root(): return lax.psum(jnp.where(mine, value, jnp.zeros_like(value)), axis)  188 us
    all_gather x2, waiting for transfers between devices, local(): lax.all_gather(partial_value.astype(jnp.bfloat16), 'aux')  72.3 us
    all_to_all x1, waiting for transfers between devices, local(): lax.all_to_all(integrals, 'occ', split_axis=2, concat_axis=0, tiled=True)  57.6 us
    all_gather x2, waiting for transfers between devices, local(): owner_whole = lax.all_gather(owner_half, 'vir', axis=3, tiled=True)  20.9 us
    dot_general x2, matrix products, local(): jnp.einsum('ijab,srjb->sria', amplitude, owner_whole, preferred_element_t...  16.7 us
    dot_general x2, matrix products, local(): jnp.einsum('sria,srjb->ijab', regrouped, owner_whole, preferred_element_t...  15.9 us
    add x1, local copies, waits for them, and re-layouts, local(): gamma_total + jnp.einsum('ijab,srjb->sria', amplitude, owner_whole, prefe...  10.2 us
  transfers between devices with their start and end apart: 6, of which 6 were waited for; matrix products, arithmetic and copies ran while one was open for 7% of the time, Pallas kernels for 0%

profile of v1, /device:TPU:0, one launch (start us, length us, event | category | flops | bytes accessed | tf_op | source)
XLA Modules:
  0.0 436.9 jit_solution(238964114244292302)
XLA Ops:
  6.5 3.6 copy.9
  10.1 0.0 copy-start.3
  10.1 6.4 %all-to-all-start = ((bf16[1,512,4,640]{3,1,0,2:T(8,128)(2,1)}), bf16[1,512,4,640]{3,1,0,2:T(8,128)(2,1)S(1)}, u32[]{:S(2)}, u32[]{:S(2)}) async-start(bf16[1,512,4,640]{3,1,0,2:T(8,128)(2,1)} %copy.9), calls=%async_computation | async-start | bytes 5242880 | tf_op jit(solution)/shard_map/all_to_all | solution.py:15
  16.5 0.0 all-reduce.3.cloned.1.call-start
  16.5 0.0 copy-done.3
  16.6 0.6 fusion.45
  18.4 57.6 %all-to-all-done = bf16[1,512,4,640]{3,1,0,2:T(8,128)(2,1)S(1)} async-done(((bf16[1,512,4,640]{3,1,0,2:T(8,128)(2,1)}), bf16[1,512,4,640]{3,1,0,2:T(8,128)(2,1)S(1)}, u32[]{:S(2)}, u32[]{:S(2)}) %all-to-all-start) | async-done | bytes 2621472 | tf_op jit(solution)/shard_map/all_to_all | solution.py:15
  76.0 2.8 fusion.30
  78.8 0.0 all-reduce.3.cloned.1.call-update
  78.8 0.0 all-gather.9.cloned.1.call-start
  78.9 188.5 %all-reduce.3.cloned.1.call-done = (bf16[4,512,1,640]{3,1,0,2:T(8,128)(2,1)}, bf16[4,512,1,640]{3,1,0,2:T(8,128)(2,1)}) async-done(((bf16[4,512,1,640]{3,1,0,2:T(8,128)(2,1)}, bf16[4,512,1,640]{3,1,0,2:T(8,128)(2,1)}), (bf16[4,512,1,640]{3,1,0,2:T(8,128)(2,1)}, bf16[4,512,1,640]{3,1,0,2:T(8,128)(2,1)})) %all-reduce.3.cloned.1.call-update) | async-done | bytes 5242896 | tf_op jit(solution)/shard_map/psum | solution.py:11
  267.3 0.0 all-gather.9.cloned.1.call-update
  267.4 0.0 all-gather.7.cloned.1.call-start
  267.4 0.7 all-gather.7.cloned.1.call-update
  268.1 0.0 all-gather.13.cloned.1.call-start
  268.2 14.9 %all-gather.9.cloned.1.call-done = bf16[4,512,1,1280]{3,1,0,2:T(8,128)(2,1)} async-done(((bf16[4,512,1,640]{3,1,0,2:T(8,128)(2,1)}), bf16[4,512,1,1280]{3,1,0,2:T(8,128)(2,1)}) %all-gather.9.cloned.1.call-update) | async-done | bytes 5242896 | tf_op jit(solution)/shard_map/all_gather | solution.py:24
  283.0 8.0 %fusion.25 = bf16[1,1,640,1280]{2,3,0,1:T(8,128)(2,1)} fusion(bf16[4,512,1,1280]{3,1,0,2:T(8,128)(2,1)} %all-gather.9.cloned.1.call-done, bf16[1,512,4,640]{3,1,0,2:T(8,128)(2,1)S(1)} %all-to-all-done), kind=kOutput, calls=%fused_computation.18 | convolution fusion | flops 3356262400 | bytes 9502720 | tf_op jit(solution)/shard_map/sria,srjb->ijab/dot_general | solution.py:26
  291.0 3.7 copy.15
  294.6 0.0 all-gather.13.cloned.1.call-update
  294.7 0.2 all-gather.11.cloned.1.call-start
  294.9 6.0 %all-gather.7.cloned.1.call-done = bf16[4,512,1,1280]{3,1,0,2:T(8,128)(2,1)} async-done(((bf16[4,512,1,640]{3,1,0,2:T(8,128)(2,1)}), bf16[4,512,1,1280]{3,1,0,2:T(8,128)(2,1)}) %all-gather.7.cloned.1.call-update) | async-done | bytes 5242896 | tf_op jit(solution)/shard_map/all_gather | solution.py:24
  300.9 8.0 %fusion.22 = bf16[1,1,640,1280]{2,3,0,1:T(8,128)(2,1)} fusion(bf16[4,512,1,1280]{3,1,0,2:T(8,128)(2,1)} %all-gather.7.cloned.1.call-done, bf16[1,512,4,640]{3,1,0,2:T(8,128)(2,1)S(1)} %all-to-all-done), kind=kOutput, calls=%fused_computation.17 | convolution fusion | flops 3356262400 | bytes 9502720 | tf_op jit(solution)/shard_map/sria,srjb->ijab/dot_general | solution.py:26
  308.9 0.0 copy-start.1
  308.9 0.0 copy-start.2
  308.9 3.8 copy.11
  312.6 0.0 all-gather.11.cloned.1.call-update
  316.4 0.0 copy-done.1
  316.4 0.7 fusion.44
  319.7 0.0 copy-done.2
  319.7 0.1 dynamic-slice_subtract_fusion.1
  319.7 30.2 %all-gather.13.cloned.1.call-done = bf16[2,1,640,1280]{3,2,1,0:T(8,128)(2,1)} async-done(((bf16[1,1,640,1280]{3,2,1,0:T(8,128)(2,1)}), bf16[2,1,640,1280]{3,2,1,0:T(8,128)(2,1)}) %all-gather.13.cloned.1.call-update) | async-done | bytes 3276816 | tf_op jit(solution)/shard_map/all_gather | solution.py:31
  349.9 3.5 reduce.5
  353.4 2.2 copy.26
  355.6 42.1 %all-gather.11.cloned.1.call-done = bf16[2,1,640,1280]{3,2,1,0:T(8,128)(2,1)} async-done(((bf16[1,1,640,1280]{3,2,1,0:T(8,128)(2,1)}), bf16[2,1,640,1280]{3,2,1,0:T(8,128)(2,1)}) %all-gather.11.cloned.1.call-update) | async-done | bytes 3276816 | tf_op jit(solution)/shard_map/all_gather | solution.py:31
  397.8 3.5 reduce.4
  401.3 2.2 copy.25
  403.5 0.0 copy-start
  403.5 7.4 %fusion = f32[4,512,640]{2,1,0:T(8,128)S(1)} fusion(bf16[4,512,1,1280]{3,1,0,2:T(8,128)(2,1)} %all-gather.9.cloned.1.call-done, bf16[640,1280]{0,1:T(8,128)(2,1)} %copy.26, f32[640]{0:T(1024)S(1)} %get-tuple-element.10, f32[1280]{0:T(1024)S(1)} %copy-done.2), kind=kOutput, calls=%fused_computation | convolution fusion | flops 3358720000 | bytes 12131840 | tf_op jit(solution)/shard_map/ijab,srjb->sria/dot_general | solution.py:34
  410.9 0.0 copy-done
  410.9 9.3 %add_bitcast_fusion = f32[4,512,1,640]{3,1,0,2:T(8,128)} fusion(f32[4,512,640]{2,1,0:T(8,128)S(1)} %fusion, bf16[4,512,1,1280]{3,1,0,2:T(8,128)(2,1)} %all-gather.7.cloned.1.call-done, bf16[640,1280]{0,1:T(8,128)(2,1)S(1)} %copy-done, f32[1280]{0:T(1024)S(1)} %copy-done.2, f32[640]{0:T(1024)S(1)} %get-tuple-element.9), kind=kOutput, calls=%fused_computation.8 | convolution fusion | flops 3360030720 | bytes 17374720 | tf_op jit(solution)/shard_map/ijab,srjb->sria/dot_general | solution.py:34
  420.2 10.2 %copy.18 = f32[4,512,1,640]{3,2,1,0:T(1,128)} copy(f32[4,512,1,640]{3,1,0,2:T(8,128)} %add_bitcast_fusion) | data formatting | bytes 10485760 | tf_op jit(solution)/shard_map/add | solution.py:34
Async XLA Ops:
  10.1 6.5 %copy-start.3 = (s32[2]{0:T(128)S(1)}, s32[2]{0:T(128)}, u32[]{:S(2)}) copy-start(s32[2]{0:T(128)} %param.7) | copy-start | bytes 28
  10.1 65.9 %all-to-all-start = ((bf16[1,512,4,640]{3,1,0,2:T(8,128)(2,1)}), bf16[1,512,4,640]{3,1,0,2:T(8,128)(2,1)S(1)}, u32[]{:S(2)}, u32[]{:S(2)}) async-start(bf16[1,512,4,640]{3,1,0,2:T(8,128)(2,1)} %copy.9), calls=%async_computation | async-start | bytes 5242880 | tf_op jit(solution)/shard_map/all_to_all | solution.py:15
  16.5 250.8 %all-reduce.3.cloned.1.call-start = ((), (), s32[]{:S(2)}) async-start(), calls=%async_computation.5 | async-start | bytes 10485760 | tf_op jit(solution)/shard_map/psum | solution.py:11
  78.8 204.2 %all-gather.9.cloned.1.call-start = ((), (), s32[]{:S(2)}) async-start(), calls=%async_computation.2 | async-start | bytes 7864320 | tf_op jit(solution)/shard_map/all_gather | solution.py:24
  267.4 33.5 %all-gather.7.cloned.1.call-start = ((), (), s32[]{:S(2)}) async-start(), calls=%async_computation.1 | async-start | bytes 7864320 | tf_op jit(solution)/shard_map/all_gather | solution.py:24
  268.1 81.8 %all-gather.13.cloned.1.call-start = ((), (), s32[]{:S(2)}) async-start(), calls=%async_computation.4 | async-start | bytes 4915200 | tf_op jit(solution)/shard_map/all_gather | solution.py:31
  294.7 103.1 %all-gather.11.cloned.1.call-start = ((), (), s32[]{:S(2)}) async-start(), calls=%async_computation.3 | async-start | bytes 4915200 | tf_op jit(solution)/shard_map/all_gather | solution.py:31
  308.9 7.5 %copy-start.1 = (f32[4]{0:T(128)S(1)}, f32[4]{0:T(128)}, u32[]{:S(2)}) copy-start(f32[4]{0:T(128)} %param.5) | copy-start | bytes 52
  308.9 10.8 %copy-start.2 = (f32[1280]{0:T(1024)S(1)}, f32[1280]{0:T(1024)}, u32[]{:S(2)}) copy-start(f32[1280]{0:T(1024)} %param.6) | copy-start | bytes 15364
  403.5 7.4 %copy-start = (bf16[640,1280]{0,1:T(8,128)(2,1)S(1)}, bf16[640,1280]{0,1:T(8,128)(2,1)}, u32[]{:S(2)}) copy-start(bf16[640,1280]{0,1:T(8,128)(2,1)} %copy.25) | copy-start | bytes 4915204
Sparse Core Ops, SparseCore 0:
  78.9 188.3 all-reduce.2
  268.9 14.0 all-gather.8
  284.6 16.2 all-gather.6
  302.3 47.5 all-gather.12
  351.3 46.3 all-gather.10
